TPU v7x, 32 devices: a whole 2x2x4 slice. The times are simulated.
32 devices in a mesh: group: 2 (over y), dev: 8 (over z, x), tp: 2 (over core).
Axes of the slice: x: 2, y: 2, z: 4, core: 2. Of those that a mesh axis runs over, the one named last changes fastest.
Arguments:
- prompt_activations: bfloat16 [4096, 8192], P(('group', 'dev')), parts along dimension 0, may hold values from -6 to 6
- key_matrix: bfloat16 [8192, 512], P('dev', 'tp'), may hold values from -0.0625 to 0.0625
- value_matrix: bfloat16 [8192, 512], P('dev', 'tp'), may hold values from -0.0625 to 0.0625
- adapter_down_keyvalue: bfloat16 [8192, 128], P('dev'), may hold values from -0.0625 to 0.0625
- adapter_up_key: bfloat16 [64, 512], P(None, 'tp'), may hold values from -1.5 to 1.5
- adapter_up_value: bfloat16 [64, 512], P(None, 'tp'), may hold values from -1.5 to 1.5
- request_adapter: int32 [16], P('group'), parts along dimension 0, may hold values from 0 to 3
- page_request: int32 [1024, 1], P('group'), parts along dimension 0, may hold values from 0 to 7; in each aligned block of 64 rows (0 to 63, 64 to 127, ...) at most 8 rows name the same one
- context_tokens: int32 [16], P('group'), parts along dimension 0, may hold values from 64 to 256
- step_query: bfloat16 [16, 4096], P(('group', 'dev'), 'tp'), parts along dimension 0, may hold values from -256 to 256
- step_key: bfloat16 [16, 512], P(('group', 'dev'), 'tp'), parts along dimension 0, may hold values from -6 to 6
- step_value: bfloat16 [16, 512], P(('group', 'dev'), 'tp'), parts along dimension 0, may hold values from -6 to 6
- stored_keys: bfloat16 [16, 256, 512], P(('group', 'dev'), None, 'tp'), parts along dimension 0, may hold values from -6 to 6
- stored_values: bfloat16 [16, 256, 512], P(('group', 'dev'), None, 'tp'), parts along dimension 0, may hold values from -6 to 6
- output_matrix: bfloat16 [4096, 8192], P('tp', 'dev'), may hold values from -0.09375 to 0.09375
- adapter_down_output: bfloat16 [4096, 64], P('tp'), may hold values from -0.09375 to 0.09375
- adapter_up_output: bfloat16 [64, 8192], P(None, 'dev'), may hold values from -1.5 to 1.5
Outputs:
- attended: bfloat16 [16, 8192], P('group', 'dev'), parts along dimension 0
There are 2 independent parts, one for each index of `group`. A program takes and returns all parts, laid end to end along the dimension named above; an argument that names none is the same for every part. Nothing has to cross between parts.
Inputs may be any that keep to these rules, and one draw needn't show every extreme that they name: `page_request`: among the pages of one device's prompt block (aligned blocks of 64 pages), no request owns more than 8; every request owns at least one page.
All inputs are finite; a program needn't handle non-finite values.
Results may differ from a plain program's by a relative error of at most 0.0086.
Values may be sent and summed in bfloat16 or wider, within the bound.
A program may use at most 64 MiB of HBM per device.

v0:
```python
import jax
import jax.numpy as jnp
from jax import lax
from jax.sharding import PartitionSpec as P

HEADS = 32
KV_HEADS = 4
HEAD = 128
LOW_RANK = 16
ADAPTER_COUNT = 4
PAGE = 4
adapter_scale = 1.0
rope_base = 500000.0


def rotate(key_rows, positions):
    row_count = key_rows.shape[0]
    blocks = key_rows.reshape(row_count, -1, HEAD)
    half_size = HEAD // 2
    exponent = jnp.arange(half_size, dtype=jnp.float32) * (2.0 / HEAD)
    frequency = jnp.exp(-jnp.log(jnp.float32(rope_base)) * exponent)
    angles = positions.astype(jnp.float32)[:, None] * frequency[None, :]
    cosine = jnp.cos(angles)[:, None, :]
    sine_part = jnp.sin(angles)[:, None, :]
    first_half = blocks[..., :half_size]
    second_half = blocks[..., half_size:]
    turned = jnp.concatenate(
        [
            first_half * cosine - second_half * sine_part,
            second_half * cosine + first_half * sine_part,
        ],
        axis=-1,
    )
    return turned.reshape(row_count, -1)


def owner_ranks(owners, row_total):
    onehot = (owners[:, None] == jnp.arange(row_total, dtype=jnp.int32)[None, :]).astype(jnp.int32)
    before = jnp.cumsum(onehot, axis=0) - onehot
    rank = jnp.sum(before * onehot, axis=1)
    return (onehot, rank)


def mask_columns(narrowed, adapter_list):
    column = jnp.arange(narrowed.shape[1], dtype=jnp.int32)
    owner = column % (ADAPTER_COUNT * LOW_RANK) // LOW_RANK
    return jnp.where(owner[None, :] == adapter_list[:, None], narrowed, jnp.zeros_like(narrowed))


def selected_narrow(activation_rows, adapter_down, adapter_list):
    narrowed = jnp.dot(activation_rows, adapter_down, preferred_element_type=jnp.float32)
    return mask_columns(narrowed, adapter_list)


def widened(selected_rows, up_key, up_value):
    split_at = ADAPTER_COUNT * LOW_RANK
    highest = lax.Precision.HIGHEST
    key_portion = jnp.dot(
        selected_rows[:, :split_at], up_key.astype(jnp.float32), precision=highest
    )
    value_portion = jnp.dot(
        selected_rows[:, split_at:], up_value.astype(jnp.float32), precision=highest
    )
    return (adapter_scale * key_portion, adapter_scale * value_portion)


def attend_local(
    query,
    old_keys,
    old_values,
    old_length,
    fresh_keys,
    fresh_values,
    fresh_valid,
    last_key,
    last_value,
):
    group_size = HEADS // KV_HEADS
    query_heads = query.reshape(-1, group_size, HEAD)
    kv_local = query_heads.shape[0]
    scale_factor = HEAD ** (-0.5)

    def score_of(key_rows):
        shaped = key_rows.reshape(key_rows.shape[0], kv_local, HEAD)
        return (
            jnp.einsum("kgd,lkd->kgl", query_heads, shaped, preferred_element_type=jnp.float32)
            * scale_factor
        )

    def mix_with(probs, value_rows):
        shaped = value_rows.reshape(value_rows.shape[0], kv_local, HEAD)
        return jnp.einsum("kgl,lkd->kgd", probs, shaped, preferred_element_type=jnp.float32)

    old_valid = jnp.arange(old_keys.shape[0], dtype=jnp.int32) < old_length
    old_scores = jnp.where(old_valid[None, None, :], score_of(old_keys), -1e30)
    fresh_scores = jnp.where(fresh_valid[None, None, :], score_of(fresh_keys), -1e30)
    last_score = score_of(last_key[None, :])
    top = jnp.maximum(
        jnp.maximum(
            jnp.max(old_scores, axis=-1, keepdims=True),
            jnp.max(fresh_scores, axis=-1, keepdims=True),
        ),
        last_score,
    )
    old_weights = jnp.exp(old_scores - top)
    fresh_weights = jnp.exp(fresh_scores - top)
    last_weight = jnp.exp(last_score - top)
    total = (
        jnp.sum(old_weights, axis=-1, keepdims=True)
        + jnp.sum(fresh_weights, axis=-1, keepdims=True)
        + last_weight
    )
    output = mix_with((old_weights / total).astype(jnp.bfloat16), old_values)
    output = output + mix_with((fresh_weights / total).astype(jnp.bfloat16), fresh_values)
    output = output + mix_with((last_weight / total).astype(jnp.bfloat16), last_value[None, :])
    return output.reshape(-1).astype(jnp.bfloat16)


def per_device(
    prompt_activations,
    key_matrix,
    value_matrix,
    adapter_down_keyvalue,
    adapter_up_key,
    adapter_up_value,
    request_adapter,
    page_request,
    context_tokens,
    step_query,
    step_key,
    step_value,
    stored_keys,
    stored_values,
    output_matrix,
    adapter_down_output,
    adapter_up_output,
):
    devices = lax.axis_size("dev")
    device = lax.axis_index("dev")
    tok_count = prompt_activations.shape[0]
    pages_here = tok_count // PAGE
    capacity = max(2, (pages_here + devices - 1) // devices)
    row_total = request_adapter.shape[0]
    owners = page_request[:, 0]
    onehot, rank = owner_ranks(owners, row_total)
    first_page = device * pages_here
    my_owners = lax.dynamic_slice_in_dim(owners, first_page, pages_here, 0)
    my_rank = lax.dynamic_slice_in_dim(rank, first_page, pages_here, 0)
    tokens = jnp.arange(tok_count, dtype=jnp.int32)
    token_page = tokens // PAGE
    token_owner = jnp.take(my_owners, token_page)
    position = (
        jnp.take(context_tokens, token_owner) + jnp.take(my_rank, token_page) * PAGE + tokens % PAGE
    )
    adapter_list = jnp.take(request_adapter, token_owner)
    key_width = key_matrix.shape[1]

    def add_rows(portion):
        return jnp.dot(prompt_activations, portion, preferred_element_type=jnp.float32)

    key_raw = add_rows(lax.all_gather(key_matrix, "dev", axis=0, tiled=True))
    value_raw = add_rows(lax.all_gather(value_matrix, "dev", axis=0, tiled=True))
    down_complete = lax.all_gather(adapter_down_keyvalue, "dev", axis=0, tiled=True)
    narrowed = jnp.dot(prompt_activations, down_complete, preferred_element_type=jnp.float32)
    selected_rows = mask_columns(narrowed, adapter_list)
    key_delta, value_delta = widened(selected_rows, adapter_up_key, adapter_up_value)
    key_rows = rotate(key_raw + key_delta, position).astype(jnp.bfloat16)
    value_rows = (value_raw + value_delta).astype(jnp.bfloat16)
    joined_rows = jnp.concatenate([key_rows, value_rows], axis=1)
    local_hot = (my_owners[:, None] == jnp.arange(row_total, dtype=jnp.int32)[None, :]).astype(
        jnp.int32
    )
    local_before = jnp.cumsum(local_hot, axis=0) - local_hot
    local_slot = jnp.sum(local_before * local_hot, axis=1)
    peer_slots = capacity * PAGE
    target = token_owner * peer_slots + jnp.take(local_slot, token_page) * PAGE + tokens % PAGE
    outgoing = (
        jnp.zeros((devices * peer_slots, 2 * key_width), jnp.bfloat16).at[target].set(joined_rows)
    )
    outgoing = outgoing.reshape(devices, peer_slots, 2 * key_width)
    incoming = lax.all_to_all(outgoing, "dev", split_axis=0, concat_axis=0, tiled=True)
    fresh_keys = incoming[:, :, :key_width].reshape(-1, key_width)
    fresh_values = incoming[:, :, key_width:].reshape(-1, key_width)
    my_column = jnp.take(onehot, device, axis=1)
    count_from = jnp.sum(my_column.reshape(devices, pages_here), axis=1)
    slot_page = jnp.arange(peer_slots, dtype=jnp.int32) // PAGE
    fresh_valid = (slot_page[None, :] < count_from[:, None]).reshape(-1)
    mixed_local = attend_local(
        step_query[0],
        stored_keys[0],
        stored_values[0],
        jnp.take(context_tokens, device),
        fresh_keys,
        fresh_values,
        fresh_valid,
        step_key[0],
        step_value[0],
    ).reshape(1, -1)
    portion = lax.all_gather(mixed_local, "dev", axis=0, tiled=True)
    plain_result = jnp.dot(portion, output_matrix, preferred_element_type=jnp.float32)
    selected_output = selected_narrow(portion, adapter_down_output, request_adapter)
    partial_output = plain_result + adapter_scale * jnp.dot(
        selected_output, adapter_up_output.astype(jnp.float32), precision=lax.Precision.HIGHEST
    )
    return lax.psum(partial_output, "tp").astype(jnp.bfloat16)


def solution(mesh):
    return jax.shard_map(
        per_device,
        mesh=mesh,
        in_specs=(
            P(("group", "dev"), None),
            P("dev", "tp"),
            P("dev", "tp"),
            P("dev", None),
            P(None, "tp"),
            P(None, "tp"),
            P("group"),
            P("group", None),
            P("group"),
            P(("group", "dev"), "tp"),
            P(("group", "dev"), "tp"),
            P(("group", "dev"), "tp"),
            P(("group", "dev"), None, "tp"),
            P(("group", "dev"), None, "tp"),
            P("tp", "dev"),
            P("tp", None),
            P(None, "dev"),
        ),
        out_specs=P("group", "dev"),
        check_vma=False,
    )
```

profile of v0, /device:TPU:0, one launch (start us, length us, event | category | flops | bytes accessed | tf_op | source)
XLA Modules:
  0.0 273.4 jit_solution(10275499087581960177)
XLA Ops:
  6.5 0.7 all-gather.7.cloned.1.call-update
  7.3 0.7 all-gather.9.cloned.1.call-update
  8.1 0.7 all-gather.5.cloned.1.call-update
  8.8 0.7 fusion.22
  9.4 1.1 reduce-window.6
  10.8 0.8 fusion.20
  11.7 0.7 dynamic-slice_bitcast_fusion
  12.4 1.9 gather_fusion
  14.3 1.9 gather_fusion.2
  16.2 0.7 fusion.21
  17.4 1.9 gather_fusion.1
  21.4 9.7 %fusion.41 = (f32[256]{0:T(256)S(1)}, s32[256]{0:T(256)S(1)}, s32[256]{0:T(256)S(1)}) fusion(s32[256]{0:T(256)S(1)} %gather_fusion.2, s32[]{:T(128)} %bitcast.19, s32[]{:T(128)} %bitcast.18, s32[]{:T(128)} %bitcast.17, s32[]{:T(128)} %bitcast.16, s32[]{:T(128)} %bitcast.15, s32[]{:T(128)} %bitcast.14, s32[]{:T(128)} %bitcast.13, s32[]{:T(128)} %bitcast.12, ...), kind=kLoop, calls=%fused_computation.94 | loop fusion | flops 15616 | bytes 6208 | tf_op jit(solution)/shard_map/convert_element_type | solution.py:22
  31.4 29.8 %all-gather.7.cloned.1.call-done = bf16[8192,128]{1,0:T(8,128)(2,1)} async-done(((bf16[1024,128]{1,0:T(8,128)(2,1)}), bf16[8192,128]{1,0:T(8,128)(2,1)}) %all-gather.7.cloned.1.call-update) | async-done | bytes 2097168 | tf_op jit(solution)/shard_map/all_gather | solution.py:163
  61.3 4.4 %convolution_select_fusion = f32[256,128]{0,1:T(8,128)S(1)} fusion(bf16[256,8192]{1,0:T(8,128)(2,1)} %param.21, bf16[8192,128]{1,0:T(8,128)(2,1)} %all-gather.7.cloned.1.call-done, s32[256]{0:T(256)S(1)} %get-tuple-element.40, s32[128]{0:T(128)S(1)} %and_select_fusion.2), kind=kOutput, calls=%fused_computation.7 | convolution fusion | flops 536936448 | bytes 6424064 | tf_op jit(solution)/shard_map/dot_general | solution.py:164
  65.6 69.1 %all-gather.9.cloned.1.call-done = bf16[8192,256]{1,0:T(8,128)(2,1)} async-done(((bf16[1024,256]{1,0:T(8,128)(2,1)}), bf16[8192,256]{1,0:T(8,128)(2,1)}) %all-gather.9.cloned.1.call-update) | async-done | bytes 4194320 | tf_op jit(solution)/shard_map/all_gather | solution.py:162
  134.7 5.2 %fusion.51 = f32[256,256]{0,1:T(8,128)S(1)} fusion(bf16[256,8192]{1,0:T(8,128)(2,1)} %param.21, bf16[8192,256]{1,0:T(8,128)(2,1)} %all-gather.9.cloned.1.call-done), kind=kOutput, calls=%fused_computation.123 | convolution fusion | flops 1073741824 | bytes 8650752 | tf_op jit(solution)/shard_map/dot_general | solution.py:159
  140.3 67.9 %all-gather.5.cloned.1.call-done = bf16[8192,256]{1,0:T(8,128)(2,1)} async-done(((bf16[1024,256]{1,0:T(8,128)(2,1)}), bf16[8192,256]{1,0:T(8,128)(2,1)}) %all-gather.5.cloned.1.call-update) | async-done | bytes 4194320 | tf_op jit(solution)/shard_map/all_gather | solution.py:161
  208.2 5.2 %fusion.50 = f32[256,256]{0,1:T(8,128)S(1)} fusion(bf16[256,8192]{1,0:T(8,128)(2,1)} %param.21, bf16[8192,256]{1,0:T(8,128)(2,1)} %all-gather.5.cloned.1.call-done), kind=kOutput, calls=%fused_computation.122 | convolution fusion | flops 1073741824 | bytes 8650752 | tf_op jit(solution)/shard_map/dot_general | solution.py:159
  214.0 2.2 scatter_custom_fusion
  216.2 3.4 %all-to-all-start = ((bf16[8,32,512]{2,1,0:T(8,128)(2,1)}), bf16[8,32,512]{2,1,0:T(8,128)(2,1)S(1)}, u32[]{:S(2)}, u32[]{:S(2)}) async-start(bf16[8,32,512]{2,1,0:T(8,128)(2,1)} %bitcast.24), calls=%async_computation | async-start | bytes 524288 | tf_op jit(solution)/shard_map/all_to_all | solution.py:181
  220.2 8.0 %all-to-all-done = bf16[8,32,512]{2,1,0:T(8,128)(2,1)S(1)} async-done(((bf16[8,32,512]{2,1,0:T(8,128)(2,1)}), bf16[8,32,512]{2,1,0:T(8,128)(2,1)S(1)}, u32[]{:S(2)}, u32[]{:S(2)}) %all-to-all-start) | async-done | bytes 262176 | tf_op jit(solution)/shard_map/all_to_all | solution.py:181
  229.2 30.5 %all-gather = bf16[8,1,2048]{2,1,0:T(2,128)(2,1)S(1)} all-gather(bf16[1,1,2048]{2,1,0:T(2,128)(2,1)S(1)} %reshape.342), channel_id=1, replica_groups=mesh['group'=2,'dev'=8,'tp'=2] {'dev'}, dimensions={0}, use_global_device_ids=true | all-gather | bytes 36864 | tf_op jit(solution)/shard_map/all_gather | solution.py:199
  259.7 2.8 %fusion.16 = f32[8,1024]{1,0:T(8,128)S(1)} fusion(bf16[2048,1024]{1,0:T(8,128)(2,1)} %param.35, bf16[8,1,2048]{2,1,0:T(2,128)(2,1)S(1)} %all-gather), kind=kOutput, calls=%fused_computation.34 | convolution fusion | flops 33554432 | bytes 4259840 | tf_op jit(solution)/shard_map/dot_general | solution.py:200
  262.9 4.0 %psum.7 = bf16[8,1024]{1,0:T(8,128)(2,1)} all-reduce(f32[8,1024]{1,0:T(8,128)S(1)} %convolution_add_fusion.2), channel_id=1, replica_groups=mesh['group'=2,'dev'=8,'tp'=2] {'tp'}, use_global_device_ids=true, to_apply=%region_11.14 | all-reduce | flops 8192 | bytes 49152 | tf_op jit(solution)/shard_map/psum | solution.py:205
  (71 shorter events, 5.5 us)
Async XLA Ops:
  6.5 256.0 %copy-start = (bf16[2048,64]{0,1:T(8,128)(2,1)S(1)}, bf16[2048,64]{0,1:T(8,128)(2,1)}, u32[]{:S(2)}) copy-start(bf16[2048,64]{0,1:T(8,128)(2,1)} %param.36) | copy-start | bytes 786436
  6.5 12.8 %copy-start.4 = (s32[8]{0:T(128)S(1)}, s32[8]{0:T(128)}, u32[]{:S(2)}) copy-start(s32[8]{0:T(128)} %param.29) | copy-start | bytes 100
  6.5 14.1 %copy-start.6 = (s32[8]{0:T(128)S(1)}, s32[8]{0:T(128)}, u32[]{:S(2)}) copy-start(s32[8]{0:T(128)} %param.27) | copy-start | bytes 100
  6.5 54.7 %all-gather.7.cloned.1.call-start = ((), (), s32[]{:S(2)}) async-start(), calls=%async_computation.2 | async-start | bytes 2359296 | tf_op jit(solution)/shard_map/all_gather | solution.py:163
  7.3 127.5 %all-gather.9.cloned.1.call-start = ((), (), s32[]{:S(2)}) async-start(), calls=%async_computation.3 | async-start | bytes 4718592 | tf_op jit(solution)/shard_map/all_gather | solution.py:162
  8.0 200.2 %all-gather.5.cloned.1.call-start = ((), (), s32[]{:S(2)}) async-start(), calls=%async_computation.1 | async-start | bytes 4718592 | tf_op jit(solution)/shard_map/all_gather | solution.py:161
  65.6 74.3 %copy-start.7 = (bf16[64,256]{1,0:T(8,128)(2,1)S(1)}, bf16[64,256]{1,0:T(8,128)(2,1)}, u32[]{:S(2)}) copy-start(bf16[64,256]{1,0:T(8,128)(2,1)} %param.26) | copy-start | bytes 98308
  140.3 73.2 %copy-start.5 = (bf16[64,256]{1,0:T(8,128)(2,1)S(1)}, bf16[64,256]{1,0:T(8,128)(2,1)}, u32[]{:S(2)}) copy-start(bf16[64,256]{1,0:T(8,128)(2,1)} %param.25) | copy-start | bytes 98308
  140.3 79.3 %copy-start.9 = (bf16[1,256]{1,0:T(2,128)(2,1)S(1)}, bf16[1,256]{1,0:T(2,128)(2,1)}, u32[]{:S(2)}) copy-start(bf16[1,256]{1,0:T(2,128)(2,1)} %param.32) | copy-start | bytes 1540
  140.3 79.4 %copy-start.1 = (bf16[1,256,256]{2,1,0:T(8,128)(2,1)S(1)}, bf16[1,256,256]{2,1,0:T(8,128)(2,1)}, u32[]{:S(2)}) copy-start(bf16[1,256,256]{2,1,0:T(8,128)(2,1)} %param.33) | copy-start | bytes 393220
  140.3 79.5 %copy-start.2 = (bf16[1,256,256]{2,1,0:T(8,128)(2,1)S(1)}, bf16[1,256,256]{2,1,0:T(8,128)(2,1)}, u32[]{:S(2)}) copy-start(bf16[1,256,256]{2,1,0:T(8,128)(2,1)} %param.34) | copy-start | bytes 393220
  140.3 79.5 %copy-start.8 = (bf16[1,2048]{1,0:T(2,128)(2,1)S(1)}, bf16[1,2048]{1,0:T(2,128)(2,1)}, u32[]{:S(2)}) copy-start(bf16[1,2048]{1,0:T(2,128)(2,1)} %param.30) | copy-start | bytes 12292
  140.3 79.5 %copy-start.10 = (bf16[1,256]{1,0:T(2,128)(2,1)S(1)}, bf16[1,256]{1,0:T(2,128)(2,1)}, u32[]{:S(2)}) copy-start(bf16[1,256]{1,0:T(2,128)(2,1)} %param.31) | copy-start | bytes 1540
  213.9 48.9 %copy-start.3 = (bf16[64,1024]{1,0:T(8,128)(2,1)S(1)}, bf16[64,1024]{1,0:T(8,128)(2,1)}, u32[]{:S(2)}) copy-start(bf16[64,1024]{1,0:T(8,128)(2,1)} %param.37) | copy-start | bytes 393220
  216.2 12.0 %all-to-all-start = ((bf16[8,32,512]{2,1,0:T(8,128)(2,1)}), bf16[8,32,512]{2,1,0:T(8,128)(2,1)S(1)}, u32[]{:S(2)}, u32[]{:S(2)}) async-start(bf16[8,32,512]{2,1,0:T(8,128)(2,1)} %bitcast.24), calls=%async_computation | async-start | bytes 524288 | tf_op jit(solution)/shard_map/all_to_all | solution.py:181
Sparse Core Ops, SparseCore 0:
  9.5 51.7 all-gather.6
  63.4 71.3 all-gather.8
  136.9 71.3 all-gather.4
where the time goes:
time: 274 us; the launch traced here: 273 us
  waiting for transfers between devices  177 us (65%)
  blocking collectives  34.5 us (13%)
  matrix products  19.5 us (7%)
  other arithmetic  14.3 us (5%)
  between operations  14 us (5%)
  local copies, waits for them, and re-layouts  10.7 us (4%)
  starting transfers between devices  3.49 us (1%)
    all_gather x1, waiting for transfers between devices, per_device(): lax.all_gather(value_matrix, 'dev', axis=0, tiled=True)  69.1 us
    all_gather x1, waiting for transfers between devices, per_device(): key_raw = add_rows(lax.all_gather(key_matrix, 'dev', axis=0, tiled=True))  67.9 us
    all_gather x1, blocking collectives, per_device(): portion = lax.all_gather(mixed_local, 'dev', axis=0, tiled=True)  30.5 us
    all_gather x1, waiting for transfers between devices, per_device(): lax.all_gather(adapter_down_keyvalue, 'dev', axis=0, tiled=True)  29.8 us
    dot_general x2, matrix products, add_rows(): jnp.dot(prompt_activations, portion, preferred_element_type=jnp.float32)  10.4 us
    convert_element_type x1, other arithmetic, rotate(): angles = positions.astype(jnp.float32)[:, None] * frequency[None, :]  9.74 us
    all_to_all x1, waiting for transfers between devices, per_device(): lax.all_to_all(outgoing, 'dev', split_axis=0, concat_axis=0, tiled=True)  8 us
  transfers between devices with their start and end apart: 4, of which 4 were waited for; matrix products, arithmetic and copies ran while one was open for 12% of the time, Pallas kernels for 0%

commit v1 on v0

--- a/solution.py
+++ b/solution.py
@@ -196,7 +196,13 @@
         step_key[0],
         step_value[0],
     ).reshape(1, -1)
-    portion = lax.all_gather(mixed_local, "dev", axis=0, tiled=True)
+    size = lax.axis_size("dev")
+    moving, shards = (mixed_local, [mixed_local])
+    for _ in range(size - 1):
+        moving = lax.ppermute(moving, "dev", [(i, (i + 1) % size) for i in range(size)])
+        shards.insert(0, moving)
+    line = jnp.concatenate(shards, axis=0)
+    portion = jnp.roll(line, (lax.axis_index("dev") + 1) * mixed_local.shape[0], axis=0)
     plain_result = jnp.dot(portion, output_matrix, preferred_element_type=jnp.float32)
     selected_output = selected_narrow(portion, adapter_down_output, request_adapter)
     partial_output = plain_result + adapter_scale * jnp.dot(

time: 274 us -> 288 us (1.051)
  waiting for transfers between devices: 177 us -> 220 us
  blocking collectives: 34.5 us -> 3.98 us
    ppermute x0 -> x7, waiting for transfers between devices: none -> 43 us  [per_device(): lax.ppermute(moving, 'dev', [(i, (i + 1) % size) for i in range(size)])]
    all_gather x1 -> x0, blocking collectives: 30.5 us -> none  [per_device(): portion = lax.all_gather(mixed_local, 'dev', axis=0, tiled=True)]
  transfers between devices with their start and end apart: 4 -> 11, of which waited for: 4 -> 11; matrix products, arithmetic and copies ran while one was open for 12% -> 11% of each run, Pallas kernels for 0% -> 0%
where the time goes in v1:
time: 288 us
  waiting for transfers between devices  220 us (76%)
  matrix products  19.5 us (7%)
  other arithmetic  14.3 us (5%)
  between operations  14 us (5%)
  local copies, waits for them, and re-layouts  10.9 us (4%)
  starting transfers between devices  4.97 us (2%)
  blocking collectives  3.98 us (1%)
    all_gather x1, waiting for transfers between devices, per_device(): lax.all_gather(value_matrix, 'dev', axis=0, tiled=True)  69.1 us
    all_gather x1, waiting for transfers between devices, per_device(): key_raw = add_rows(lax.all_gather(key_matrix, 'dev', axis=0, tiled=True))  67.9 us
    ppermute x7, waiting for transfers between devices, per_device(): lax.ppermute(moving, 'dev', [(i, (i + 1) % size) for i in range(size)])  43 us
    all_gather x1, waiting for transfers between devices, per_device(): lax.all_gather(adapter_down_keyvalue, 'dev', axis=0, tiled=True)  29.8 us
    dot_general x2, matrix products, add_rows(): jnp.dot(prompt_activations, portion, preferred_element_type=jnp.float32)  10.4 us
    convert_element_type x1, other arithmetic, rotate(): angles = positions.astype(jnp.float32)[:, None] * frequency[None, :]  9.74 us
    all_to_all x1, waiting for transfers between devices, per_device(): lax.all_to_all(outgoing, 'dev', split_axis=0, concat_axis=0, tiled=True)  8 us
  transfers between devices with their start and end apart: 11, of which 11 were waited for; matrix products, arithmetic and copies ran while one was open for 11% of the time, Pallas kernels for 0%

profile of v1, /device:TPU:0, one launch (start us, length us, event | category | flops | bytes accessed | tf_op | source)
XLA Modules:
  0.0 287.6 jit_solution(12283344256710790057)
XLA Ops:
  9.4 1.1 reduce-window.6
  12.4 1.9 gather_fusion
  14.3 1.9 gather_fusion.2
  17.4 1.9 gather_fusion.1
  21.4 9.7 %fusion.38 = (f32[256]{0:T(256)S(1)}, s32[256]{0:T(256)S(1)}) fusion(s32[256]{0:T(256)S(1)} %gather_fusion.2, s32[]{:T(128)} %bitcast.19, s32[]{:T(128)} %bitcast.18, s32[]{:T(128)} %bitcast.17, s32[]{:T(128)} %bitcast.16, s32[]{:T(128)} %bitcast.15, s32[]{:T(128)} %bitcast.14, s32[]{:T(128)} %bitcast.13, s32[]{:T(128)} %bitcast.12, s32[256]{0:T(256)S(1)} %gather_fusion, ...), kind=kLoop, calls=%fused_computation.91 | loop fusion | flops 13568 | bytes 4160 | tf_op jit(solution)/shard_map/convert_element_type | solution.py:22
  31.4 29.8 %all-gather.6.cloned.1.call-done = bf16[8192,128]{1,0:T(8,128)(2,1)} async-done(((bf16[1024,128]{1,0:T(8,128)(2,1)}), bf16[8192,128]{1,0:T(8,128)(2,1)}) %all-gather.6.cloned.1.call-update) | async-done | bytes 2097168 | tf_op jit(solution)/shard_map/all_gather | solution.py:163
  61.3 4.4 %convolution_select_fusion = f32[256,128]{0,1:T(8,128)S(1)} fusion(bf16[256,8192]{1,0:T(8,128)(2,1)} %param.21, bf16[8192,128]{1,0:T(8,128)(2,1)} %all-gather.6.cloned.1.call-done, s32[256]{0:T(256)S(1)} %get-tuple-element.40, s32[128]{0:T(128)S(1)} %and_select_fusion.2), kind=kOutput, calls=%fused_computation.7 | convolution fusion | flops 536936448 | bytes 6424064 | tf_op jit(solution)/shard_map/dot_general | solution.py:164
  65.6 69.1 %all-gather.8.cloned.1.call-done = bf16[8192,256]{1,0:T(8,128)(2,1)} async-done(((bf16[1024,256]{1,0:T(8,128)(2,1)}), bf16[8192,256]{1,0:T(8,128)(2,1)}) %all-gather.8.cloned.1.call-update) | async-done | bytes 4194320 | tf_op jit(solution)/shard_map/all_gather | solution.py:162
  134.7 5.2 %fusion.51 = f32[256,256]{0,1:T(8,128)S(1)} fusion(bf16[256,8192]{1,0:T(8,128)(2,1)} %param.21, bf16[8192,256]{1,0:T(8,128)(2,1)} %all-gather.8.cloned.1.call-done), kind=kOutput, calls=%fused_computation.123 | convolution fusion | flops 1073741824 | bytes 8650752 | tf_op jit(solution)/shard_map/dot_general | solution.py:159
  140.3 67.9 %all-gather.4.cloned.1.call-done = bf16[8192,256]{1,0:T(8,128)(2,1)} async-done(((bf16[1024,256]{1,0:T(8,128)(2,1)}), bf16[8192,256]{1,0:T(8,128)(2,1)}) %all-gather.4.cloned.1.call-update) | async-done | bytes 4194320 | tf_op jit(solution)/shard_map/all_gather | solution.py:161
  208.2 5.2 %fusion.50 = f32[256,256]{0,1:T(8,128)S(1)} fusion(bf16[256,8192]{1,0:T(8,128)(2,1)} %param.21, bf16[8192,256]{1,0:T(8,128)(2,1)} %all-gather.4.cloned.1.call-done), kind=kOutput, calls=%fused_computation.122 | convolution fusion | flops 1073741824 | bytes 8650752 | tf_op jit(solution)/shard_map/dot_general | solution.py:159
  214.0 2.2 scatter_custom_fusion
  216.2 3.4 %all-to-all-start = ((bf16[8,32,512]{2,1,0:T(8,128)(2,1)}), bf16[8,32,512]{2,1,0:T(8,128)(2,1)S(1)}, u32[]{:S(2)}, u32[]{:S(2)}) async-start(bf16[8,32,512]{2,1,0:T(8,128)(2,1)} %bitcast.24), calls=%async_computation | async-start | bytes 524288 | tf_op jit(solution)/shard_map/all_to_all | solution.py:181
  220.2 8.0 %all-to-all-done = bf16[8,32,512]{2,1,0:T(8,128)(2,1)S(1)} async-done(((bf16[8,32,512]{2,1,0:T(8,128)(2,1)}), bf16[8,32,512]{2,1,0:T(8,128)(2,1)S(1)}, u32[]{:S(2)}, u32[]{:S(2)}) %all-to-all-start) | async-done | bytes 262176 | tf_op jit(solution)/shard_map/all_to_all | solution.py:181
  229.2 1.5 collective-permute-start
  230.6 4.9 %collective-permute-done = bf16[1,2048]{1,0:T(2,128)(2,1)S(1)} collective-permute-done((bf16[1,2048]{1,0:T(2,128)(2,1)S(1)}, bf16[1,2048]{1,0:T(2,128)(2,1)S(1)}, u32[]{:S(2)}, u32[]{:S(2)}) %collective-permute-start) | collective-permute-done | bytes 4128 | tf_op jit(solution)/shard_map/ppermute | solution.py:202
  235.6 6.3 %collective-permute-done.1 = bf16[1,2048]{1,0:T(2,128)(2,1)S(1)} collective-permute-done((bf16[1,2048]{1,0:T(2,128)(2,1)S(1)}, bf16[1,2048]{1,0:T(2,128)(2,1)S(1)}, u32[]{:S(2)}, u32[]{:S(2)}) %collective-permute-start.1) | collective-permute-done | bytes 4128 | tf_op jit(solution)/shard_map/ppermute | solution.py:202
  241.9 6.3 %collective-permute-done.2 = bf16[1,2048]{1,0:T(2,128)(2,1)S(1)} collective-permute-done((bf16[1,2048]{1,0:T(2,128)(2,1)S(1)}, bf16[1,2048]{1,0:T(2,128)(2,1)S(1)}, u32[]{:S(2)}, u32[]{:S(2)}) %collective-permute-start.2) | collective-permute-done | bytes 4128 | tf_op jit(solution)/shard_map/ppermute | solution.py:202
  248.3 6.3 %collective-permute-done.3 = bf16[1,2048]{1,0:T(2,128)(2,1)S(1)} collective-permute-done((bf16[1,2048]{1,0:T(2,128)(2,1)S(1)}, bf16[1,2048]{1,0:T(2,128)(2,1)S(1)}, u32[]{:S(2)}, u32[]{:S(2)}) %collective-permute-start.3) | collective-permute-done | bytes 4128 | tf_op jit(solution)/shard_map/ppermute | solution.py:202
  254.6 6.3 %collective-permute-done.4 = bf16[1,2048]{1,0:T(2,128)(2,1)S(1)} collective-permute-done((bf16[1,2048]{1,0:T(2,128)(2,1)S(1)}, bf16[1,2048]{1,0:T(2,128)(2,1)S(1)}, u32[]{:S(2)}, u32[]{:S(2)}) %collective-permute-start.4) | collective-permute-done | bytes 4128 | tf_op jit(solution)/shard_map/ppermute | solution.py:202
  261.0 6.3 %collective-permute-done.5 = bf16[1,2048]{1,0:T(2,128)(2,1)S(1)} collective-permute-done((bf16[1,2048]{1,0:T(2,128)(2,1)S(1)}, bf16[1,2048]{1,0:T(2,128)(2,1)S(1)}, u32[]{:S(2)}, u32[]{:S(2)}) %collective-permute-start.5) | collective-permute-done | bytes 4128 | tf_op jit(solution)/shard_map/ppermute | solution.py:202
  267.3 6.3 %collective-permute-done.6 = bf16[1,2048]{1,0:T(2,128)(2,1)S(1)} collective-permute-done((bf16[1,2048]{1,0:T(2,128)(2,1)S(1)}, bf16[1,2048]{1,0:T(2,128)(2,1)S(1)}, u32[]{:S(2)}, u32[]{:S(2)}) %collective-permute-start.6) | collective-permute-done | bytes 4128 | tf_op jit(solution)/shard_map/ppermute | solution.py:202
  274.2 2.9 convolution_add_fusion.2
  277.1 4.0 %psum.7 = bf16[8,1024]{1,0:T(8,128)(2,1)} all-reduce(f32[8,1024]{1,0:T(8,128)S(1)} %convolution_add_fusion.2), channel_id=1, replica_groups=mesh['group'=2,'dev'=8,'tp'=2] {'tp'}, use_global_device_ids=true, to_apply=%region_11.14 | all-reduce | flops 8192 | bytes 49152 | tf_op jit(solution)/shard_map/psum | solution.py:211
  (86 shorter events, 10.7 us)
Async XLA Ops:
  6.5 267.3 %copy-start = (bf16[2048,64]{0,1:T(8,128)(2,1)S(1)}, bf16[2048,64]{0,1:T(8,128)(2,1)}, u32[]{:S(2)}) copy-start(bf16[2048,64]{0,1:T(8,128)(2,1)} %param.36) | copy-start | bytes 786436
  6.5 12.8 %copy-start.5 = (s32[8]{0:T(128)S(1)}, s32[8]{0:T(128)}, u32[]{:S(2)}) copy-start(s32[8]{0:T(128)} %param.29) | copy-start | bytes 100
  6.5 14.1 %copy-start.4 = (s32[8]{0:T(128)S(1)}, s32[8]{0:T(128)}, u32[]{:S(2)}) copy-start(s32[8]{0:T(128)} %param.27) | copy-start | bytes 100
  6.5 54.7 %all-gather.6.cloned.1.call-start = ((), (), s32[]{:S(2)}) async-start(), calls=%async_computation.2 | async-start | bytes 2359296 | tf_op jit(solution)/shard_map/all_gather | solution.py:163
  7.3 127.5 %all-gather.8.cloned.1.call-start = ((), (), s32[]{:S(2)}) async-start(), calls=%async_computation.3 | async-start | bytes 4718592 | tf_op jit(solution)/shard_map/all_gather | solution.py:162
  8.0 200.2 %all-gather.4.cloned.1.call-start = ((), (), s32[]{:S(2)}) async-start(), calls=%async_computation.1 | async-start | bytes 4718592 | tf_op jit(solution)/shard_map/all_gather | solution.py:161
  65.6 74.3 %copy-start.7 = (bf16[64,256]{1,0:T(8,128)(2,1)S(1)}, bf16[64,256]{1,0:T(8,128)(2,1)}, u32[]{:S(2)}) copy-start(bf16[64,256]{1,0:T(8,128)(2,1)} %param.26) | copy-start | bytes 98308
  140.3 73.2 %copy-start.6 = (bf16[64,256]{1,0:T(8,128)(2,1)S(1)}, bf16[64,256]{1,0:T(8,128)(2,1)}, u32[]{:S(2)}) copy-start(bf16[64,256]{1,0:T(8,128)(2,1)} %param.25) | copy-start | bytes 98308
  140.3 79.3 %copy-start.9 = (bf16[1,256]{1,0:T(2,128)(2,1)S(1)}, bf16[1,256]{1,0:T(2,128)(2,1)}, u32[]{:S(2)}) copy-start(bf16[1,256]{1,0:T(2,128)(2,1)} %param.32) | copy-start | bytes 1540
  140.3 79.4 %copy-start.1 = (bf16[1,256,256]{2,1,0:T(8,128)(2,1)S(1)}, bf16[1,256,256]{2,1,0:T(8,128)(2,1)}, u32[]{:S(2)}) copy-start(bf16[1,256,256]{2,1,0:T(8,128)(2,1)} %param.33) | copy-start | bytes 393220
  140.3 79.5 %copy-start.2 = (bf16[1,256,256]{2,1,0:T(8,128)(2,1)S(1)}, bf16[1,256,256]{2,1,0:T(8,128)(2,1)}, u32[]{:S(2)}) copy-start(bf16[1,256,256]{2,1,0:T(8,128)(2,1)} %param.34) | copy-start | bytes 393220
  140.3 79.5 %copy-start.8 = (bf16[1,2048]{1,0:T(2,128)(2,1)S(1)}, bf16[1,2048]{1,0:T(2,128)(2,1)}, u32[]{:S(2)}) copy-start(bf16[1,2048]{1,0:T(2,128)(2,1)} %param.30) | copy-start | bytes 12292
  140.3 79.5 %copy-start.10 = (bf16[1,256]{1,0:T(2,128)(2,1)S(1)}, bf16[1,256]{1,0:T(2,128)(2,1)}, u32[]{:S(2)}) copy-start(bf16[1,256]{1,0:T(2,128)(2,1)} %param.31) | copy-start | bytes 1540
  213.5 60.6 %copy-start.3 = (bf16[64,1024]{1,0:T(8,128)(2,1)S(1)}, bf16[64,1024]{1,0:T(8,128)(2,1)}, u32[]{:S(2)}) copy-start(bf16[64,1024]{1,0:T(8,128)(2,1)} %param.37) | copy-start | bytes 393220
  216.2 12.0 %all-to-all-start = ((bf16[8,32,512]{2,1,0:T(8,128)(2,1)}), bf16[8,32,512]{2,1,0:T(8,128)(2,1)S(1)}, u32[]{:S(2)}, u32[]{:S(2)}) async-start(bf16[8,32,512]{2,1,0:T(8,128)(2,1)} %bitcast.24), calls=%async_computation | async-start | bytes 524288 | tf_op jit(solution)/shard_map/all_to_all | solution.py:181
  229.2 6.4 %collective-permute-start = (bf16[1,2048]{1,0:T(2,128)(2,1)S(1)}, bf16[1,2048]{1,0:T(2,128)(2,1)S(1)}, u32[]{:S(2)}, u32[]{:S(2)}) collective-permute-start(bf16[1,2048]{1,0:T(2,128)(2,1)S(1)} %convert_element_type.59), channel_id=1, source_target_pairs={{0,2},{2,4},{4,6},{6,8},{8,10},{10,12},{12,14},{14,0},{1,3},{3,5},... | collective-permute-start | bytes 12296 | tf_op jit(solution)/shard_map/ppermute | solution.py:202
  235.6 6.3 %collective-permute-start.1 = (bf16[1,2048]{1,0:T(2,128)(2,1)S(1)}, bf16[1,2048]{1,0:T(2,128)(2,1)S(1)}, u32[]{:S(2)}, u32[]{:S(2)}) collective-permute-start(bf16[1,2048]{1,0:T(2,128)(2,1)S(1)} %collective-permute-done), channel_id=1, source_target_pairs={{0,2},{2,4},{4,6},{6,8},{8,10},{10,12},{12,14},{14,0},{1,3},{3,5},... | collective-permute-start | bytes 12296 | tf_op jit(solution)/shard_map/ppermute | solution.py:202
  241.9 6.3 %collective-permute-start.2 = (bf16[1,2048]{1,0:T(2,128)(2,1)S(1)}, bf16[1,2048]{1,0:T(2,128)(2,1)S(1)}, u32[]{:S(2)}, u32[]{:S(2)}) collective-permute-start(bf16[1,2048]{1,0:T(2,128)(2,1)S(1)} %collective-permute-done.1), channel_id=1, source_target_pairs={{0,2},{2,4},{4,6},{6,8},{8,10},{10,12},{12,14},{14,0},{1,3},{3,5},... | collective-permute-start | bytes 12296 | tf_op jit(solution)/shard_map/ppermute | solution.py:202
  248.3 6.3 %collective-permute-start.3 = (bf16[1,2048]{1,0:T(2,128)(2,1)S(1)}, bf16[1,2048]{1,0:T(2,128)(2,1)S(1)}, u32[]{:S(2)}, u32[]{:S(2)}) collective-permute-start(bf16[1,2048]{1,0:T(2,128)(2,1)S(1)} %collective-permute-done.2), channel_id=1, source_target_pairs={{0,2},{2,4},{4,6},{6,8},{8,10},{10,12},{12,14},{14,0},{1,3},{3,5},... | collective-permute-start | bytes 12296 | tf_op jit(solution)/shard_map/ppermute | solution.py:202
  254.6 6.3 %collective-permute-start.4 = (bf16[1,2048]{1,0:T(2,128)(2,1)S(1)}, bf16[1,2048]{1,0:T(2,128)(2,1)S(1)}, u32[]{:S(2)}, u32[]{:S(2)}) collective-permute-start(bf16[1,2048]{1,0:T(2,128)(2,1)S(1)} %collective-permute-done.3), channel_id=1, source_target_pairs={{0,2},{2,4},{4,6},{6,8},{8,10},{10,12},{12,14},{14,0},{1,3},{3,5},... | collective-permute-start | bytes 12296 | tf_op jit(solution)/shard_map/ppermute | solution.py:202
  261.0 6.3 %collective-permute-start.5 = (bf16[1,2048]{1,0:T(2,128)(2,1)S(1)}, bf16[1,2048]{1,0:T(2,128)(2,1)S(1)}, u32[]{:S(2)}, u32[]{:S(2)}) collective-permute-start(bf16[1,2048]{1,0:T(2,128)(2,1)S(1)} %collective-permute-done.4), channel_id=1, source_target_pairs={{0,2},{2,4},{4,6},{6,8},{8,10},{10,12},{12,14},{14,0},{1,3},{3,5},... | collective-permute-start | bytes 12296 | tf_op jit(solution)/shard_map/ppermute | solution.py:202
  267.3 6.3 %collective-permute-start.6 = (bf16[1,2048]{1,0:T(2,128)(2,1)S(1)}, bf16[1,2048]{1,0:T(2,128)(2,1)S(1)}, u32[]{:S(2)}, u32[]{:S(2)}) collective-permute-start(bf16[1,2048]{1,0:T(2,128)(2,1)S(1)} %collective-permute-done.5), channel_id=1, source_target_pairs={{0,2},{2,4},{4,6},{6,8},{8,10},{10,12},{12,14},{14,0},{1,3},{3,5},... | collective-permute-start | bytes 12296 | tf_op jit(solution)/shard_map/ppermute | solution.py:202
Sparse Core Ops, SparseCore 0:
  9.5 51.7 all-gather.5
  63.4 71.3 all-gather.7
  136.9 71.3 all-gather.3
